TPU v7x, 512 devices: a whole 4x8x8 slice. The times are simulated.
512 devices in a mesh: ctx: 64 (over z, x, core), head: 8 (over y).
Axes of the slice: x: 4, y: 8, z: 8, core: 2. Of those that a mesh axis runs over, the one named last changes fastest.
Arguments:
- queries: bfloat16 [16384, 4096], P(('ctx', 'head')), may hold values from -6 to 6
- key_rows: bfloat16 [16384, 4096], P(('ctx', 'head')), may hold values from -6 to 6
- value_rows: bfloat16 [16384, 4096], P(('ctx', 'head')), may hold values from -6 to 6
- grad_out: bfloat16 [16384, 4096], P(('ctx', 'head')), may hold values from -6 to 6
Outputs:
- grad_query: bfloat16 [16384, 4096], P(('ctx', 'head'))
- grad_key: bfloat16 [16384, 4096], P(('ctx', 'head'))
- grad_value: bfloat16 [16384, 4096], P(('ctx', 'head'))
All inputs are finite; a program needn't handle non-finite values.
Results may differ from a plain program's by a relative error of at most 0.0021.
Values may be sent and summed in bfloat16 or wider, within the bound.
A program may use at most 128 MiB of HBM per device.

v0:
```python
import jax
import jax.numpy as jnp
from jax import lax
from jax.sharding import PartitionSpec as P

HEAD_DIM = 128
GROUP = 128


def exclusive_scans(forward_part, backward_part, axis):
    count = lax.axis_size(axis)
    fwd_total, fwd_excl = (forward_part, jnp.zeros_like(forward_part))
    bwd_total, bwd_excl = (backward_part, jnp.zeros_like(backward_part))
    shift = 1
    while shift < count:
        to_right = [(i, i + shift) for i in range(count - shift)]
        to_left = [(i + shift, i) for i in range(count - shift)]
        got_fwd = lax.ppermute(fwd_total, axis, to_right)
        got_bwd = lax.ppermute(bwd_total, axis, to_left)
        fwd_excl = fwd_excl + got_fwd
        bwd_excl = bwd_excl + got_bwd
        if shift * 2 < count:
            fwd_total = fwd_total + got_fwd
            bwd_total = bwd_total + got_bwd
        shift *= 2
    return (fwd_excl, bwd_excl)


def per_device(queries, key_rows, value_rows, grad_out):
    stacked = jnp.stack([queries, key_rows, value_rows, grad_out])
    q_all, k_all, v_all, d_all = lax.all_to_all(
        stacked, "head", split_axis=2, concat_axis=1, tiled=True
    )
    rows_here = q_all.shape[0]
    heads_here = q_all.shape[1] // HEAD_DIM
    scale = (HEAD_DIM * rows_here * lax.axis_size("ctx")) ** (-0.5)
    highest = lax.Precision.HIGHEST
    block = GROUP
    nblocks = rows_here // block
    shape_four = (nblocks, block, heads_here, HEAD_DIM)
    q_four = q_all.reshape(shape_four)
    k_four = k_all.reshape(shape_four)
    v_four = v_all.reshape(shape_four)
    d_four = d_all.reshape(shape_four)
    kv_blocks = jnp.einsum("ntha,nthb->nhab", v_four, k_four, preferred_element_type=jnp.float32)
    g_blocks = jnp.einsum("ntha,nthb->nhab", d_four, q_four, preferred_element_type=jnp.float32)
    kv_local = jnp.sum(kv_blocks, axis=0)
    g_local = jnp.sum(g_blocks, axis=0)
    kv_before, g_after = exclusive_scans(kv_local, g_local, "ctx")
    row_ids = lax.broadcasted_iota(jnp.int32, (nblocks, nblocks), 0)
    col_ids = lax.broadcasted_iota(jnp.int32, (nblocks, nblocks), 1)
    strict_lower = (col_ids < row_ids).astype(jnp.float32)
    strict_upper = (col_ids > row_ids).astype(jnp.float32)
    kv_in = kv_before[None] + jnp.einsum(
        "mn,nhab->mhab", strict_lower, kv_blocks, precision=highest
    )
    g_in = g_after[None] + jnp.einsum("mn,nhab->mhab", strict_upper, g_blocks, precision=highest)
    later = lax.broadcasted_iota(jnp.int32, (block, block), 0)
    earlier = lax.broadcasted_iota(jnp.int32, (block, block), 1)
    causal = (later >= earlier).astype(jnp.float32)
    scores = (
        jnp.einsum("nthd,nshd->nhts", q_four, k_four, preferred_element_type=jnp.float32)
        * (scale * causal)
    ).astype(jnp.bfloat16)
    dscores = (
        jnp.einsum("nthd,nshd->nhts", d_four, v_four, preferred_element_type=jnp.float32) * causal
    ).astype(jnp.bfloat16)
    k_float = k_four.astype(jnp.float32)
    v_float = v_four.astype(jnp.float32)
    d_float = d_four.astype(jnp.float32)
    grad_q = scale * (
        jnp.einsum("nhts,nshd->nthd", dscores, k_four, preferred_element_type=jnp.float32)
        + jnp.einsum("ntha,nhab->nthb", d_float, kv_in, precision=highest)
    )
    grad_k = scale * (
        jnp.einsum("nhts,nthd->nshd", dscores, q_four, preferred_element_type=jnp.float32)
        + jnp.einsum("ntha,nhab->nthb", v_float, g_in, precision=highest)
    )
    grad_v = jnp.einsum(
        "nhts,nthd->nshd", scores, d_four, preferred_element_type=jnp.float32
    ) + scale * jnp.einsum("nthb,nhab->ntha", k_float, g_in, precision=highest)
    flat_shape = (rows_here, heads_here * HEAD_DIM)
    grad_q = grad_q.reshape(flat_shape).astype(jnp.bfloat16)
    grad_k = grad_k.reshape(flat_shape).astype(jnp.bfloat16)
    grad_v = grad_v.reshape(flat_shape).astype(jnp.bfloat16)
    grads = jnp.stack([grad_q, grad_k, grad_v])
    result_q, result_k, result_v = lax.all_to_all(
        grads, "head", split_axis=1, concat_axis=2, tiled=True
    )
    return (result_q, result_k, result_v)


def solution(mesh):
    placed = (
        P(("ctx", "head"), None),
        P(("ctx", "head"), None),
        P(("ctx", "head"), None),
        P(("ctx", "head"), None),
    )
    return jax.shard_map(
        per_device,
        mesh=mesh,
        in_specs=placed,
        out_specs=(P(("ctx", "head"), None), P(("ctx", "head"), None), P(("ctx", "head"), None)),
        check_vma=False,
    )
```

profile of v0, /device:TPU:6, one launch (start us, length us, event | category | flops | bytes accessed | tf_op | source)
XLA Modules:
  0.0 192.5 jit_solution(13614894121044651994)
XLA Ops:
  0.6 1.3 pad_maximum_fusion
  2.0 4.7 %copy.93 = bf16[4,32,4096]{1,0,2:T(4,128)(2,1)} copy(bf16[4,32,4096]{2,1,0:T(8,128)(2,1)S(1)} %pad_maximum_fusion) | data formatting | bytes 2097152 | tf_op jit(solution)/shard_map/stack | solution.py:30
  6.6 7.0 %reshape.73 = bf16[8,2,32768]{2,1,0:T(2,128)(2,1)S(1)} reshape(bf16[4096,4,32]{2,1,0:T(4,128)(2,1)} %bitcast.57) | data formatting | bytes 2097152
  13.6 35.6 %all_to_all.30 = bf16[8,2,32768]{2,1,0:T(2,128)(2,1)S(1)} all-to-all(bf16[8,2,32768]{2,1,0:T(2,128)(2,1)S(1)} %reshape.73), channel_id=1, replica_groups=mesh['ctx'=64,'head'=8] {'head'}, dimensions={0} | all-to-all | bytes 2097152 | tf_op jit(solution)/shard_map/all_to_all | solution.py:31
  49.2 4.5 %reshape.74 = bf16[4096,4,32]{2,1,0:T(4,128)(2,1)} reshape(bf16[8,2,32768]{2,1,0:T(2,128)(2,1)S(1)} %all_to_all.30) | data formatting | bytes 2097152
  53.7 5.5 %copy.94 = bf16[4,32,8,512]{3,1,2,0:T(8,128)(2,1)S(1)} copy(bf16[4,32,8,512]{1,0,3,2:T(4,128)(2,1)} %bitcast.58) | data formatting | bytes 2097152 | tf_op jit(solution)/shard_map/all_to_all | solution.py:31
  59.5 0.3 fusion.55
  59.8 1.9 collective-permute-start
  62.0 0.2 fusion.54
  62.3 3.6 %collective-permute-start.6 = (f32[4,128,128]{2,1,0:T(8,128)S(1)}, f32[4,128,128]{2,1,0:T(8,128)S(1)}, u32[]{:S(2)}, u32[]{:S(2)}) collective-permute-start(f32[4,128,128]{2,1,0:T(8,128)S(1)} %get-tuple-element.10), channel_id=1, source_target_pairs={{8,0},{16,8},{24,16},{32,24},{40,32},{48,40},{56,48},{64,56},{72,6... | collective-permute-start | bytes 786440 | tf_op jit(solution)/shard_map/ppermute | solution.py:19
  65.9 1.5 collective-permute-done
  67.5 6.3 %collective-permute-start.1 = (f32[4,128,128]{2,1,0:T(8,128)S(1)}, f32[4,128,128]{2,1,0:T(8,128)S(1)}, u32[]{:S(2)}, u32[]{:S(2)}) collective-permute-start(f32[4,128,128]{2,1,0:T(8,128)S(1)} %add.88), channel_id=1, source_target_pairs={{0,16},{8,24},{16,32},{24,40},{32,48},{40,56},{48,64},{56,72},{64,... | collective-permute-start | bytes 786440 | tf_op jit(solution)/shard_map/ppermute | solution.py:18
  73.9 1.9 collective-permute-start.7
  75.8 1.9 collective-permute-done.1
  77.7 4.2 %collective-permute-start.2 = (f32[4,128,128]{2,1,0:T(8,128)S(1)}, f32[4,128,128]{2,1,0:T(8,128)S(1)}, u32[]{:S(2)}, u32[]{:S(2)}) collective-permute-start(f32[4,128,128]{2,1,0:T(8,128)S(1)} %add.90), channel_id=1, source_target_pairs={{0,32},{8,40},{16,48},{24,56},{32,64},{40,72},{48,80},{56,88},{64,... | collective-permute-start | bytes 786440 | tf_op jit(solution)/shard_map/ppermute | solution.py:18
  81.9 8.9 %collective-permute-done.7 = f32[4,128,128]{2,1,0:T(8,128)S(1)} collective-permute-done((f32[4,128,128]{2,1,0:T(8,128)S(1)}, f32[4,128,128]{2,1,0:T(8,128)S(1)}, u32[]{:S(2)}, u32[]{:S(2)}) %collective-permute-start.7) | collective-permute-done | bytes 262176 | tf_op jit(solution)/shard_map/ppermute | solution.py:19
  90.9 1.9 collective-permute-start.8
  92.8 4.3 %collective-permute-start.3 = (f32[4,128,128]{2,1,0:T(8,128)S(1)}, f32[4,128,128]{2,1,0:T(8,128)S(1)}, u32[]{:S(2)}, u32[]{:S(2)}) collective-permute-start(f32[4,128,128]{2,1,0:T(8,128)S(1)} %add.92), channel_id=1, source_target_pairs={{0,64},{8,72},{16,80},{24,88},{32,96},{40,104},{48,112},{56,120},{... | collective-permute-start | bytes 786440 | tf_op jit(solution)/shard_map/ppermute | solution.py:18
  97.2 5.4 %collective-permute-done.8 = f32[4,128,128]{2,1,0:T(8,128)S(1)} collective-permute-done((f32[4,128,128]{2,1,0:T(8,128)S(1)}, f32[4,128,128]{2,1,0:T(8,128)S(1)}, u32[]{:S(2)}, u32[]{:S(2)}) %collective-permute-start.8) | collective-permute-done | bytes 262176 | tf_op jit(solution)/shard_map/ppermute | solution.py:19
  102.6 1.3 collective-permute-start.9
  103.9 7.7 %collective-permute-start.4 = (f32[4,128,128]{2,1,0:T(8,128)S(1)}, f32[4,128,128]{2,1,0:T(8,128)S(1)}, u32[]{:S(2)}, u32[]{:S(2)}) collective-permute-start(f32[4,128,128]{2,1,0:T(8,128)S(1)} %add.94), channel_id=1, source_target_pairs={{0,128},{8,136},{16,144},{24,152},{32,160},{40,168},{48,176},{56,1... | collective-permute-start | bytes 786440 | tf_op jit(solution)/shard_map/ppermute | solution.py:18
  111.7 0.3 fusion.4
  112.0 1.3 collective-permute-start.10
  113.3 2.3 %collective-permute-done.4 = f32[4,128,128]{2,1,0:T(8,128)S(1)} collective-permute-done((f32[4,128,128]{2,1,0:T(8,128)S(1)}, f32[4,128,128]{2,1,0:T(8,128)S(1)}, u32[]{:S(2)}, u32[]{:S(2)}) %collective-permute-start.4) | collective-permute-done | bytes 262176 | tf_op jit(solution)/shard_map/ppermute | solution.py:18
  115.7 19.5 %collective-permute-start.5 = (f32[4,128,128]{2,1,0:T(8,128)S(1)}, f32[4,128,128]{2,1,0:T(8,128)S(1)}, u32[]{:S(2)}, u32[]{:S(2)}) collective-permute-start(f32[4,128,128]{2,1,0:T(8,128)S(1)} %add.96), channel_id=1, source_target_pairs={{0,256},{8,264},{16,272},{24,280},{32,288},{40,296},{48,304},{56,3... | collective-permute-start | bytes 786440 | tf_op jit(solution)/shard_map/ppermute | solution.py:18
  135.3 0.3 fusion.28
  135.6 0.3 fusion.18
  135.9 0.7 copy-done.2
  136.6 0.7 add.109
  137.3 1.3 collective-permute-start.11
  138.6 2.4 %collective-permute-done.5 = f32[4,128,128]{2,1,0:T(8,128)S(1)} collective-permute-done((f32[4,128,128]{2,1,0:T(8,128)S(1)}, f32[4,128,128]{2,1,0:T(8,128)S(1)}, u32[]{:S(2)}, u32[]{:S(2)}) %collective-permute-start.5) | collective-permute-done | bytes 262176 | tf_op jit(solution)/shard_map/ppermute | solution.py:18
  141.1 1.4 broadcast_add_fusion.1
  142.5 0.6 fusion.9
  143.1 0.2 copy.103
  143.3 0.8 convert_element_type.70
  144.1 9.8 %collective-permute-done.11 = f32[4,128,128]{2,1,0:T(8,128)} collective-permute-done((f32[4,128,128]{2,1,0:T(8,128)}, f32[4,128,128]{2,1,0:T(8,128)}, u32[]{:S(2)}, u32[]{:S(2)}) %collective-permute-start.11) | collective-permute-done | bytes 262176 | tf_op jit(solution)/shard_map/ppermute | solution.py:19
  153.9 1.3 add_add_fusion
  155.2 1.4 broadcast_add_fusion
  156.6 0.7 convolution_multiply_fusion.2
  157.2 0.6 fusion.8
  157.8 0.2 copy.110
  158.2 0.5 fusion.7
  158.7 0.2 copy.116
  159.1 0.7 copy.117
  159.8 30.3 %all_to_all.31 = bf16[3,256,512]{2,0,1:T(4,128)(2,1)S(1)} all-to-all(bf16[3,256,512]{2,0,1:T(4,128)(2,1)S(1)} %copy.117), channel_id=1, replica_groups=mesh['ctx'=64,'head'=8] {'head'}, dimensions={1} | all-to-all | bytes 1572864 | tf_op jit(solution)/shard_map/all_to_all | solution.py:87
  190.4 0.7 copy.124
  191.1 0.7 copy.125
  191.8 0.7 copy.126
  (35 shorter events, 1.6 us)
Async XLA Ops:
  59.8 7.7 %collective-permute-start = (f32[4,128,128]{2,1,0:T(8,128)S(1)}, f32[4,128,128]{2,1,0:T(8,128)S(1)}, u32[]{:S(2)}, u32[]{:S(2)}) collective-permute-start(f32[4,128,128]{2,1,0:T(8,128)S(1)} %get-tuple-element.12), channel_id=1, source_target_pairs={{0,8},{8,16},{16,24},{24,32},{32,40},{40,48},{48,56},{56,64},{64,7... | collective-permute-start | bytes 786440 | tf_op jit(solution)/shard_map/ppermute | solution.py:18
  62.3 11.5 %collective-permute-start.6 = (f32[4,128,128]{2,1,0:T(8,128)S(1)}, f32[4,128,128]{2,1,0:T(8,128)S(1)}, u32[]{:S(2)}, u32[]{:S(2)}) collective-permute-start(f32[4,128,128]{2,1,0:T(8,128)S(1)} %get-tuple-element.10), channel_id=1, source_target_pairs={{8,0},{16,8},{24,16},{32,24},{40,32},{48,40},{56,48},{64,56},{72,6... | collective-permute-start | bytes 786440 | tf_op jit(solution)/shard_map/ppermute | solution.py:19
  67.5 10.2 %collective-permute-start.1 = (f32[4,128,128]{2,1,0:T(8,128)S(1)}, f32[4,128,128]{2,1,0:T(8,128)S(1)}, u32[]{:S(2)}, u32[]{:S(2)}) collective-permute-start(f32[4,128,128]{2,1,0:T(8,128)S(1)} %add.88), channel_id=1, source_target_pairs={{0,16},{8,24},{16,32},{24,40},{32,48},{40,56},{48,64},{56,72},{64,... | collective-permute-start | bytes 786440 | tf_op jit(solution)/shard_map/ppermute | solution.py:18
  73.9 17.0 %collective-permute-start.7 = (f32[4,128,128]{2,1,0:T(8,128)S(1)}, f32[4,128,128]{2,1,0:T(8,128)S(1)}, u32[]{:S(2)}, u32[]{:S(2)}) collective-permute-start(f32[4,128,128]{2,1,0:T(8,128)S(1)} %add.101), channel_id=1, source_target_pairs={{16,0},{24,8},{32,16},{40,24},{48,32},{56,40},{64,48},{72,56},{80,... | collective-permute-start | bytes 786440 | tf_op jit(solution)/shard_map/ppermute | solution.py:19
  77.7 15.1 %collective-permute-start.2 = (f32[4,128,128]{2,1,0:T(8,128)S(1)}, f32[4,128,128]{2,1,0:T(8,128)S(1)}, u32[]{:S(2)}, u32[]{:S(2)}) collective-permute-start(f32[4,128,128]{2,1,0:T(8,128)S(1)} %add.90), channel_id=1, source_target_pairs={{0,32},{8,40},{16,48},{24,56},{32,64},{40,72},{48,80},{56,88},{64,... | collective-permute-start | bytes 786440 | tf_op jit(solution)/shard_map/ppermute | solution.py:18
  90.9 11.7 %collective-permute-start.8 = (f32[4,128,128]{2,1,0:T(8,128)S(1)}, f32[4,128,128]{2,1,0:T(8,128)S(1)}, u32[]{:S(2)}, u32[]{:S(2)}) collective-permute-start(f32[4,128,128]{2,1,0:T(8,128)S(1)} %add.103), channel_id=1, source_target_pairs={{32,0},{40,8},{48,16},{56,24},{64,32},{72,40},{80,48},{88,56},{96,... | collective-permute-start | bytes 786440 | tf_op jit(solution)/shard_map/ppermute | solution.py:19
  92.8 11.0 %collective-permute-start.3 = (f32[4,128,128]{2,1,0:T(8,128)S(1)}, f32[4,128,128]{2,1,0:T(8,128)S(1)}, u32[]{:S(2)}, u32[]{:S(2)}) collective-permute-start(f32[4,128,128]{2,1,0:T(8,128)S(1)} %add.92), channel_id=1, source_target_pairs={{0,64},{8,72},{16,80},{24,88},{32,96},{40,104},{48,112},{56,120},{... | collective-permute-start | bytes 786440 | tf_op jit(solution)/shard_map/ppermute | solution.py:18
  102.5 9.1 %copy-start = (f32[4,128,128]{2,1,0:T(8,128)}, f32[4,128,128]{2,1,0:T(8,128)S(1)}, u32[]{:S(2)}) copy-start(f32[4,128,128]{2,1,0:T(8,128)S(1)} %collective-permute-done.8) | copy-start | bytes 786436
  102.6 9.4 %collective-permute-start.9 = (f32[4,128,128]{2,1,0:T(8,128)S(1)}, f32[4,128,128]{2,1,0:T(8,128)S(1)}, u32[]{:S(2)}, u32[]{:S(2)}) collective-permute-start(f32[4,128,128]{2,1,0:T(8,128)S(1)} %add.105), channel_id=1, source_target_pairs={{64,0},{72,8},{80,16},{88,24},{96,32},{104,40},{112,48},{120,56},{... | collective-permute-start | bytes 786440 | tf_op jit(solution)/shard_map/ppermute | solution.py:19
  103.9 11.8 %collective-permute-start.4 = (f32[4,128,128]{2,1,0:T(8,128)S(1)}, f32[4,128,128]{2,1,0:T(8,128)S(1)}, u32[]{:S(2)}, u32[]{:S(2)}) collective-permute-start(f32[4,128,128]{2,1,0:T(8,128)S(1)} %add.94), channel_id=1, source_target_pairs={{0,128},{8,136},{16,144},{24,152},{32,160},{40,168},{48,176},{56,1... | collective-permute-start | bytes 786440 | tf_op jit(solution)/shard_map/ppermute | solution.py:18
  112.0 23.9 %copy-start.1 = (f32[4,128,128]{2,1,0:T(8,128)}, f32[4,128,128]{2,1,0:T(8,128)S(1)}, u32[]{:S(2)}) copy-start(f32[4,128,128]{2,1,0:T(8,128)S(1)} %collective-permute-done.9) | copy-start | bytes 786436
  112.0 23.8 %collective-permute-start.10 = (f32[4,128,128]{2,1,0:T(8,128)S(1)}, f32[4,128,128]{2,1,0:T(8,128)S(1)}, u32[]{:S(2)}, u32[]{:S(2)}) collective-permute-start(f32[4,128,128]{2,1,0:T(8,128)S(1)} %add.107), channel_id=1, source_target_pairs={{128,0},{136,8},{144,16},{152,24},{160,32},{168,40},{176,48},{184,... | collective-permute-start | bytes 786440 | tf_op jit(solution)/shard_map/ppermute | solution.py:19
  115.7 25.3 %collective-permute-start.5 = (f32[4,128,128]{2,1,0:T(8,128)S(1)}, f32[4,128,128]{2,1,0:T(8,128)S(1)}, u32[]{:S(2)}, u32[]{:S(2)}) collective-permute-start(f32[4,128,128]{2,1,0:T(8,128)S(1)} %add.96), channel_id=1, source_target_pairs={{0,256},{8,264},{16,272},{24,280},{32,288},{40,296},{48,304},{56,3... | collective-permute-start | bytes 786440 | tf_op jit(solution)/shard_map/ppermute | solution.py:18
  135.9 0.7 copy-start.2
  137.3 16.6 %collective-permute-start.11 = (f32[4,128,128]{2,1,0:T(8,128)}, f32[4,128,128]{2,1,0:T(8,128)}, u32[]{:S(2)}, u32[]{:S(2)}) collective-permute-start(f32[4,128,128]{2,1,0:T(8,128)} %add.109), channel_id=1, source_target_pairs={{256,0},{264,8},{272,16},{280,24},{288,32},{296,40},{304,48},{312,... | collective-permute-start | bytes 786440 | tf_op jit(solution)/shard_map/ppermute | solution.py:19
  155.2 3.8 %copy-start.3 = (bf16[1,256,512]{2,1,0:T(8,128)(2,1)S(1)}, bf16[1,256,512]{2,1,0:T(8,128)(2,1)}, u32[]{:S(2)}) copy-start(bf16[1,256,512]{2,1,0:T(8,128)(2,1)} %convert_element_type.70) | copy-start | bytes 786436
where the time goes:
time: 193 us
  blocking collectives  66 us (34%)
  starting transfers between devices  55.3 us (29%)
  waiting for transfers between devices  32.2 us (17%)
  local copies, waits for them, and re-layouts  27.6 us (14%)
  matrix products  6.56 us (3%)
  other arithmetic  3.85 us (2%)
    ppermute x6, starting transfers between devices, exclusive_scans(): got_fwd = lax.ppermute(fwd_total, axis, to_right)  43.9 us
    all_to_all x1, blocking collectives, per_device(): lax.all_to_all(stacked, 'head', split_axis=2, concat_axis=1, tiled=True)  35.6 us
    all_to_all x1, blocking collectives, per_device(): lax.all_to_all(grads, 'head', split_axis=1, concat_axis=2, tiled=True)  30.3 us
    ppermute x6, waiting for transfers between devices, exclusive_scans(): got_bwd = lax.ppermute(bwd_total, axis, to_left)  24.1 us
    unnamed x13, local copies, waits for them, and re-layouts  14.3 us
    ppermute x6, starting transfers between devices, exclusive_scans(): got_bwd = lax.ppermute(bwd_total, axis, to_left)  11.3 us
    ppermute x6, waiting for transfers between devices, exclusive_scans(): got_fwd = lax.ppermute(fwd_total, axis, to_right)  8.12 us
    all_to_all x1, local copies, waits for them, and re-layouts, per_device(): lax.all_to_all(stacked, 'head', split_axis=2, concat_axis=1, tiled=True)  5.51 us
  transfers between devices with their start and end apart: 12, of which 7 were waited for; matrix products, arithmetic and copies ran while one was open for 3% of the time, Pallas kernels for 0%

commit v1 on v0

--- a/solution.py
+++ b/solution.py
@@ -5,6 +5,28 @@
 
 HEAD_DIM = 128
 GROUP = 128
+
+
+def trees_name(obj):
+    response = lax.axis_size("head")
+    step_out = lax.axis_index("head")
+    local_out, seen_now = (response, step_out)
+    r_now = obj.shape[2] // local_out
+    u_next = list(obj.shape)
+    u_next[2] = r_now
+    oldest = u_next[1]
+    u_next[1] = oldest * local_out
+    main = jnp.zeros(u_next, obj.dtype)
+    tick = 0
+    while tick < local_out:
+        carry = lax.dynamic_slice_in_dim(obj, (seen_now ^ tick) * r_now, r_now, axis=2)
+        if tick:
+            carry = lax.ppermute(
+                carry, axis_name="head", perm=[(p, p ^ tick) for p in range(local_out)]
+            )
+        main = lax.dynamic_update_slice_in_dim(main, carry, (seen_now ^ tick) * oldest, axis=1)
+        tick = tick + 1
+    return main
 
 
 def exclusive_scans(forward_part, backward_part, axis):
@@ -28,9 +50,7 @@
 
 def per_device(queries, key_rows, value_rows, grad_out):
     stacked = jnp.stack([queries, key_rows, value_rows, grad_out])
-    q_all, k_all, v_all, d_all = lax.all_to_all(
-        stacked, "head", split_axis=2, concat_axis=1, tiled=True
-    )
+    q_all, k_all, v_all, d_all = trees_name(stacked)
     rows_here = q_all.shape[0]
     heads_here = q_all.shape[1] // HEAD_DIM
     scale = (HEAD_DIM * rows_here * lax.axis_size("ctx")) ** (-0.5)

time: 193 us -> 171 us (0.89)
  the two profiles are of different devices: /device:TPU:6 before, /device:TPU:66 now
where the time goes in v1:
time: 171 us; the launch traced here: 170 us
  starting transfers between devices  78.3 us (46%)
  waiting for transfers between devices  46.2 us (27%)
  blocking collectives  31 us (18%)
  matrix products  6.56 us (4%)
  local copies, waits for them, and re-layouts  4.81 us (3%)
  other arithmetic  1.97 us (1%)
    ppermute x6, starting transfers between devices, exclusive_scans(): got_fwd = lax.ppermute(fwd_total, axis, to_right)  35.6 us
    all_to_all x1, blocking collectives, per_device(): lax.all_to_all(grads, 'head', split_axis=1, concat_axis=2, tiled=True)  31 us
    ppermute x7, starting transfers between devices, trees_name(): lax.ppermute(carry, axis_name='head', perm=[(p, p ^ tick) for p in range(...  27.4 us
    ppermute x6, waiting for transfers between devices, exclusive_scans(): got_bwd = lax.ppermute(bwd_total, axis, to_left)  21.8 us
    ppermute x6, starting transfers between devices, exclusive_scans(): got_bwd = lax.ppermute(bwd_total, axis, to_left)  15.2 us
    ppermute x7, waiting for transfers between devices, trees_name(): lax.ppermute(carry, axis_name='head', perm=[(p, p ^ tick) for p in range(...  13.7 us
    ppermute x6, waiting for transfers between devices, exclusive_scans(): got_fwd = lax.ppermute(fwd_total, axis, to_right)  10.7 us
  transfers between devices with their start and end apart: 19, of which 13 were waited for; matrix products, arithmetic and copies ran while one was open for 2% of the time, Pallas kernels for 0%

profile of v1, /device:TPU:66, one launch (start us, length us, event | category | flops | bytes accessed | tf_op | source)
XLA Modules:
  0.0 170.1 jit_solution(14607141227536725315)
XLA Ops:
  0.7 1.3 pad_maximum_fusion
  2.2 3.5 %collective-permute-start = (bf16[4,32,512]{2,1,0:T(8,128)(2,1)S(1)}, bf16[4,32,512]{2,1,0:T(8,128)(2,1)S(1)}, u32[]{:S(2)}, u32[]{:S(2)}) collective-permute-start(bf16[4,32,512]{2,1,0:T(8,128)(2,1)S(1)} %get-tuple-element.13), channel_id=1, source_target_pairs={{0,1},{1,0},{2,3},{3,2},{4,5},{5,4},{6,7},{7,6},{8,9},{9,8},{10,11... | collective-permute-start | bytes 393224 | tf_op jit(solution)/shard_map/ppermute | solution.py:24
  5.7 4.5 %collective-permute-start.1 = (bf16[4,32,512]{2,1,0:T(8,128)(2,1)S(1)}, bf16[4,32,512]{2,1,0:T(8,128)(2,1)S(1)}, u32[]{:S(2)}, u32[]{:S(2)}) collective-permute-start(bf16[4,32,512]{2,1,0:T(8,128)(2,1)S(1)} %get-tuple-element.12), channel_id=1, source_target_pairs={{0,2},{1,3},{2,0},{3,1},{4,6},{5,7},{6,4},{7,5},{8,10},{9,11},{10,... | collective-permute-start | bytes 393224 | tf_op jit(solution)/shard_map/ppermute | solution.py:24
  10.2 2.1 %collective-permute-start.2 = (bf16[4,32,512]{2,1,0:T(8,128)(2,1)S(1)}, bf16[4,32,512]{2,1,0:T(8,128)(2,1)S(1)}, u32[]{:S(2)}, u32[]{:S(2)}) collective-permute-start(bf16[4,32,512]{2,1,0:T(8,128)(2,1)S(1)} %get-tuple-element.11), channel_id=1, source_target_pairs={{0,3},{1,2},{2,1},{3,0},{4,7},{5,6},{6,5},{7,4},{8,11},{9,10},{10,... | collective-permute-start | bytes 393224 | tf_op jit(solution)/shard_map/ppermute | solution.py:24
  12.4 7.7 %collective-permute-start.3 = (bf16[4,32,512]{2,1,0:T(8,128)(2,1)S(1)}, bf16[4,32,512]{2,1,0:T(8,128)(2,1)S(1)}, u32[]{:S(2)}, u32[]{:S(2)}) collective-permute-start(bf16[4,32,512]{2,1,0:T(8,128)(2,1)S(1)} %get-tuple-element.10), channel_id=1, source_target_pairs={{0,4},{1,5},{2,6},{3,7},{4,0},{5,1},{6,2},{7,3},{8,12},{9,13},{10,... | collective-permute-start | bytes 393224 | tf_op jit(solution)/shard_map/ppermute | solution.py:24
  20.1 1.9 %collective-permute-start.4 = (bf16[4,32,512]{2,1,0:T(8,128)(2,1)S(1)}, bf16[4,32,512]{2,1,0:T(8,128)(2,1)S(1)}, u32[]{:S(2)}, u32[]{:S(2)}) collective-permute-start(bf16[4,32,512]{2,1,0:T(8,128)(2,1)S(1)} %get-tuple-element.9), channel_id=1, source_target_pairs={{0,5},{1,4},{2,7},{3,6},{4,1},{5,0},{6,3},{7,2},{8,13},{9,12},{10,... | collective-permute-start | bytes 393224 | tf_op jit(solution)/shard_map/ppermute | solution.py:24
  22.1 5.5 %collective-permute-start.5 = (bf16[4,32,512]{2,1,0:T(8,128)(2,1)S(1)}, bf16[4,32,512]{2,1,0:T(8,128)(2,1)S(1)}, u32[]{:S(2)}, u32[]{:S(2)}) collective-permute-start(bf16[4,32,512]{2,1,0:T(8,128)(2,1)S(1)} %get-tuple-element.8), channel_id=1, source_target_pairs={{0,6},{1,7},{2,4},{3,5},{4,2},{5,3},{6,0},{7,1},{8,14},{9,15},{10,... | collective-permute-start | bytes 393224 | tf_op jit(solution)/shard_map/ppermute | solution.py:24
  27.6 2.2 %collective-permute-start.6 = (bf16[4,32,512]{2,1,0:T(8,128)(2,1)S(1)}, bf16[4,32,512]{2,1,0:T(8,128)(2,1)S(1)}, u32[]{:S(2)}, u32[]{:S(2)}) collective-permute-start(bf16[4,32,512]{2,1,0:T(8,128)(2,1)S(1)} %get-tuple-element.7), channel_id=1, source_target_pairs={{0,7},{1,6},{2,5},{3,4},{4,3},{5,2},{6,1},{7,0},{8,15},{9,14},{10,... | collective-permute-start | bytes 393224 | tf_op jit(solution)/shard_map/ppermute | solution.py:24
  29.9 5.6 %collective-permute-done.4 = bf16[4,32,512]{2,1,0:T(8,128)(2,1)S(1)} collective-permute-done((bf16[4,32,512]{2,1,0:T(8,128)(2,1)S(1)}, bf16[4,32,512]{2,1,0:T(8,128)(2,1)S(1)}, u32[]{:S(2)}, u32[]{:S(2)}) %collective-permute-start.4) | collective-permute-done | bytes 131104 | tf_op jit(solution)/shard_map/ppermute | solution.py:24
  35.5 2.9 %collective-permute-done.5 = bf16[4,32,512]{2,1,0:T(8,128)(2,1)S(1)} collective-permute-done((bf16[4,32,512]{2,1,0:T(8,128)(2,1)S(1)}, bf16[4,32,512]{2,1,0:T(8,128)(2,1)S(1)}, u32[]{:S(2)}, u32[]{:S(2)}) %collective-permute-start.5) | collective-permute-done | bytes 131104 | tf_op jit(solution)/shard_map/ppermute | solution.py:24
  38.3 5.2 %collective-permute-done.6 = bf16[4,32,512]{2,1,0:T(8,128)(2,1)S(1)} collective-permute-done((bf16[4,32,512]{2,1,0:T(8,128)(2,1)S(1)}, bf16[4,32,512]{2,1,0:T(8,128)(2,1)S(1)}, u32[]{:S(2)}, u32[]{:S(2)}) %collective-permute-start.6) | collective-permute-done | bytes 131104 | tf_op jit(solution)/shard_map/ppermute | solution.py:24
  44.2 1.9 %collective-permute-start.13 = (f32[4,128,128]{2,1,0:T(8,128)S(1)}, f32[4,128,128]{2,1,0:T(8,128)S(1)}, u32[]{:S(2)}, u32[]{:S(2)}) collective-permute-start(f32[4,128,128]{2,1,0:T(8,128)S(1)} %get-tuple-element.18), channel_id=1, source_target_pairs={{8,0},{16,8},{24,16},{32,24},{40,32},{48,40},{56,48},{64,56},{72,6... | collective-permute-start | bytes 786440 | tf_op jit(solution)/shard_map/ppermute | solution.py:41
  46.3 0.3 fusion.55
  46.6 2.4 %collective-permute-start.7 = (f32[4,128,128]{2,1,0:T(8,128)S(1)}, f32[4,128,128]{2,1,0:T(8,128)S(1)}, u32[]{:S(2)}, u32[]{:S(2)}) collective-permute-start(f32[4,128,128]{2,1,0:T(8,128)S(1)} %get-tuple-element.20), channel_id=1, source_target_pairs={{0,8},{8,16},{16,24},{24,32},{32,40},{40,48},{48,56},{56,64},{64,7... | collective-permute-start | bytes 786440 | tf_op jit(solution)/shard_map/ppermute | solution.py:40
  49.0 1.1 collective-permute-done.13
  50.1 3.8 %collective-permute-start.14 = (f32[4,128,128]{2,1,0:T(8,128)S(1)}, f32[4,128,128]{2,1,0:T(8,128)S(1)}, u32[]{:S(2)}, u32[]{:S(2)}) collective-permute-start(f32[4,128,128]{2,1,0:T(8,128)S(1)} %add.165), channel_id=1, source_target_pairs={{16,0},{24,8},{32,16},{40,24},{48,32},{56,40},{64,48},{72,56},{80,... | collective-permute-start | bytes 786440 | tf_op jit(solution)/shard_map/ppermute | solution.py:41
  53.9 0.5 collective-permute-done.7
  54.4 3.4 %collective-permute-start.8 = (f32[4,128,128]{2,1,0:T(8,128)S(1)}, f32[4,128,128]{2,1,0:T(8,128)S(1)}, u32[]{:S(2)}, u32[]{:S(2)}) collective-permute-start(f32[4,128,128]{2,1,0:T(8,128)S(1)} %add.152), channel_id=1, source_target_pairs={{0,16},{8,24},{16,32},{24,40},{32,48},{40,56},{48,64},{56,72},{64,... | collective-permute-start | bytes 786440 | tf_op jit(solution)/shard_map/ppermute | solution.py:40
  57.8 2.3 %collective-permute-done.14 = f32[4,128,128]{2,1,0:T(8,128)S(1)} collective-permute-done((f32[4,128,128]{2,1,0:T(8,128)S(1)}, f32[4,128,128]{2,1,0:T(8,128)S(1)}, u32[]{:S(2)}, u32[]{:S(2)}) %collective-permute-start.14) | collective-permute-done | bytes 262176 | tf_op jit(solution)/shard_map/ppermute | solution.py:41
  60.1 5.0 %collective-permute-start.15 = (f32[4,128,128]{2,1,0:T(8,128)S(1)}, f32[4,128,128]{2,1,0:T(8,128)S(1)}, u32[]{:S(2)}, u32[]{:S(2)}) collective-permute-start(f32[4,128,128]{2,1,0:T(8,128)S(1)} %add.167), channel_id=1, source_target_pairs={{32,0},{40,8},{48,16},{56,24},{64,32},{72,40},{80,48},{88,56},{96,... | collective-permute-start | bytes 786440 | tf_op jit(solution)/shard_map/ppermute | solution.py:41
  65.2 1.3 collective-permute-done.8
  66.5 5.8 %collective-permute-start.9 = (f32[4,128,128]{2,1,0:T(8,128)S(1)}, f32[4,128,128]{2,1,0:T(8,128)S(1)}, u32[]{:S(2)}, u32[]{:S(2)}) collective-permute-start(f32[4,128,128]{2,1,0:T(8,128)S(1)} %add.154), channel_id=1, source_target_pairs={{0,32},{8,40},{16,48},{24,56},{32,64},{40,72},{48,80},{56,88},{64,... | collective-permute-start | bytes 786440 | tf_op jit(solution)/shard_map/ppermute | solution.py:40
  72.3 0.2 collective-permute-done.15
  72.6 1.9 %collective-permute-start.16 = (f32[4,128,128]{2,1,0:T(8,128)S(1)}, f32[4,128,128]{2,1,0:T(8,128)S(1)}, u32[]{:S(2)}, u32[]{:S(2)}) collective-permute-start(f32[4,128,128]{2,1,0:T(8,128)S(1)} %add.169), channel_id=1, source_target_pairs={{64,0},{72,8},{80,16},{88,24},{96,32},{104,40},{112,48},{120,56},{... | collective-permute-start | bytes 786440 | tf_op jit(solution)/shard_map/ppermute | solution.py:41
  74.5 4.8 %collective-permute-done.9 = f32[4,128,128]{2,1,0:T(8,128)S(1)} collective-permute-done((f32[4,128,128]{2,1,0:T(8,128)S(1)}, f32[4,128,128]{2,1,0:T(8,128)S(1)}, u32[]{:S(2)}, u32[]{:S(2)}) %collective-permute-start.9) | collective-permute-done | bytes 262176 | tf_op jit(solution)/shard_map/ppermute | solution.py:40
  79.3 4.3 %collective-permute-start.10 = (f32[4,128,128]{2,1,0:T(8,128)S(1)}, f32[4,128,128]{2,1,0:T(8,128)S(1)}, u32[]{:S(2)}, u32[]{:S(2)}) collective-permute-start(f32[4,128,128]{2,1,0:T(8,128)S(1)} %add.156), channel_id=1, source_target_pairs={{0,64},{8,72},{16,80},{24,88},{32,96},{40,104},{48,112},{56,120},{... | collective-permute-start | bytes 786440 | tf_op jit(solution)/shard_map/ppermute | solution.py:40
  83.6 0.2 collective-permute-done.16
  83.9 1.3 collective-permute-start.17
  85.2 4.2 %collective-permute-done.10 = f32[4,128,128]{2,1,0:T(8,128)S(1)} collective-permute-done((f32[4,128,128]{2,1,0:T(8,128)S(1)}, f32[4,128,128]{2,1,0:T(8,128)S(1)}, u32[]{:S(2)}, u32[]{:S(2)}) %collective-permute-start.10) | collective-permute-done | bytes 262176 | tf_op jit(solution)/shard_map/ppermute | solution.py:40
  89.5 11.2 %collective-permute-start.11 = (f32[4,128,128]{2,1,0:T(8,128)S(1)}, f32[4,128,128]{2,1,0:T(8,128)S(1)}, u32[]{:S(2)}, u32[]{:S(2)}) collective-permute-start(f32[4,128,128]{2,1,0:T(8,128)S(1)} %add.158), channel_id=1, source_target_pairs={{0,128},{8,136},{16,144},{24,152},{32,160},{40,168},{48,176},{56,1... | collective-permute-start | bytes 786440 | tf_op jit(solution)/shard_map/ppermute | solution.py:40
  100.7 9.5 %collective-permute-done.17 = f32[4,128,128]{2,1,0:T(8,128)S(1)} collective-permute-done((f32[4,128,128]{2,1,0:T(8,128)S(1)}, f32[4,128,128]{2,1,0:T(8,128)S(1)}, u32[]{:S(2)}, u32[]{:S(2)}) %collective-permute-start.17) | collective-permute-done | bytes 262176 | tf_op jit(solution)/shard_map/ppermute | solution.py:41
  110.2 1.3 collective-permute-start.18
  111.6 0.3 fusion.4
  111.9 8.5 %collective-permute-start.12 = (f32[4,128,128]{2,1,0:T(8,128)S(1)}, f32[4,128,128]{2,1,0:T(8,128)S(1)}, u32[]{:S(2)}, u32[]{:S(2)}) collective-permute-start(f32[4,128,128]{2,1,0:T(8,128)S(1)} %add.160), channel_id=1, source_target_pairs={{0,256},{8,264},{16,272},{24,280},{32,288},{40,296},{48,304},{56,3... | collective-permute-start | bytes 786440 | tf_op jit(solution)/shard_map/ppermute | solution.py:40
  120.4 8.5 %collective-permute-done.18 = f32[4,128,128]{2,1,0:T(8,128)S(1)} collective-permute-done((f32[4,128,128]{2,1,0:T(8,128)S(1)}, f32[4,128,128]{2,1,0:T(8,128)S(1)}, u32[]{:S(2)}, u32[]{:S(2)}) %collective-permute-start.18) | collective-permute-done | bytes 262176 | tf_op jit(solution)/shard_map/ppermute | solution.py:41
  129.0 1.4 broadcast_add_fusion
  130.4 0.6 fusion.16
  131.0 0.7 convolution_multiply_fusion.2
  131.8 1.4 broadcast_add_fusion.1
  133.2 0.6 fusion.10
  133.8 0.3 fusion.9
  134.4 0.3 fusion.8
  135.0 0.5 fusion.7
  135.9 0.7 copy.81
  136.6 31.0 %all_to_all.15 = bf16[3,256,512]{2,0,1:T(4,128)(2,1)S(1)} all-to-all(bf16[3,256,512]{2,0,1:T(4,128)(2,1)S(1)} %copy.81), channel_id=1, replica_groups=mesh['ctx'=64,'head'=8] {'head'}, dimensions={1} | all-to-all | bytes 1572864 | tf_op jit(solution)/shard_map/all_to_all | solution.py:107
  167.9 0.7 copy.88
  168.6 0.7 copy.89
  169.3 0.7 copy.90
  (45 shorter events, 2.8 us)
Async XLA Ops:
  2.2 19.9 %collective-permute-start = (bf16[4,32,512]{2,1,0:T(8,128)(2,1)S(1)}, bf16[4,32,512]{2,1,0:T(8,128)(2,1)S(1)}, u32[]{:S(2)}, u32[]{:S(2)}) collective-permute-start(bf16[4,32,512]{2,1,0:T(8,128)(2,1)S(1)} %get-tuple-element.13), channel_id=1, source_target_pairs={{0,1},{1,0},{2,3},{3,2},{4,5},{5,4},{6,7},{7,6},{8,9},{9,8},{10,11... | collective-permute-start | bytes 393224 | tf_op jit(solution)/shard_map/ppermute | solution.py:24
  5.7 21.9 %collective-permute-start.1 = (bf16[4,32,512]{2,1,0:T(8,128)(2,1)S(1)}, bf16[4,32,512]{2,1,0:T(8,128)(2,1)S(1)}, u32[]{:S(2)}, u32[]{:S(2)}) collective-permute-start(bf16[4,32,512]{2,1,0:T(8,128)(2,1)S(1)} %get-tuple-element.12), channel_id=1, source_target_pairs={{0,2},{1,3},{2,0},{3,1},{4,6},{5,7},{6,4},{7,5},{8,10},{9,11},{10,... | collective-permute-start | bytes 393224 | tf_op jit(solution)/shard_map/ppermute | solution.py:24
  10.2 19.6 %collective-permute-start.2 = (bf16[4,32,512]{2,1,0:T(8,128)(2,1)S(1)}, bf16[4,32,512]{2,1,0:T(8,128)(2,1)S(1)}, u32[]{:S(2)}, u32[]{:S(2)}) collective-permute-start(bf16[4,32,512]{2,1,0:T(8,128)(2,1)S(1)} %get-tuple-element.11), channel_id=1, source_target_pairs={{0,3},{1,2},{2,1},{3,0},{4,7},{5,6},{6,5},{7,4},{8,11},{9,10},{10,... | collective-permute-start | bytes 393224 | tf_op jit(solution)/shard_map/ppermute | solution.py:24
  12.4 17.5 %collective-permute-start.3 = (bf16[4,32,512]{2,1,0:T(8,128)(2,1)S(1)}, bf16[4,32,512]{2,1,0:T(8,128)(2,1)S(1)}, u32[]{:S(2)}, u32[]{:S(2)}) collective-permute-start(bf16[4,32,512]{2,1,0:T(8,128)(2,1)S(1)} %get-tuple-element.10), channel_id=1, source_target_pairs={{0,4},{1,5},{2,6},{3,7},{4,0},{5,1},{6,2},{7,3},{8,12},{9,13},{10,... | collective-permute-start | bytes 393224 | tf_op jit(solution)/shard_map/ppermute | solution.py:24
  20.1 15.4 %collective-permute-start.4 = (bf16[4,32,512]{2,1,0:T(8,128)(2,1)S(1)}, bf16[4,32,512]{2,1,0:T(8,128)(2,1)S(1)}, u32[]{:S(2)}, u32[]{:S(2)}) collective-permute-start(bf16[4,32,512]{2,1,0:T(8,128)(2,1)S(1)} %get-tuple-element.9), channel_id=1, source_target_pairs={{0,5},{1,4},{2,7},{3,6},{4,1},{5,0},{6,3},{7,2},{8,13},{9,12},{10,... | collective-permute-start | bytes 393224 | tf_op jit(solution)/shard_map/ppermute | solution.py:24
  22.1 16.2 %collective-permute-start.5 = (bf16[4,32,512]{2,1,0:T(8,128)(2,1)S(1)}, bf16[4,32,512]{2,1,0:T(8,128)(2,1)S(1)}, u32[]{:S(2)}, u32[]{:S(2)}) collective-permute-start(bf16[4,32,512]{2,1,0:T(8,128)(2,1)S(1)} %get-tuple-element.8), channel_id=1, source_target_pairs={{0,6},{1,7},{2,4},{3,5},{4,2},{5,3},{6,0},{7,1},{8,14},{9,15},{10,... | collective-permute-start | bytes 393224 | tf_op jit(solution)/shard_map/ppermute | solution.py:24
  27.6 16.0 %collective-permute-start.6 = (bf16[4,32,512]{2,1,0:T(8,128)(2,1)S(1)}, bf16[4,32,512]{2,1,0:T(8,128)(2,1)S(1)}, u32[]{:S(2)}, u32[]{:S(2)}) collective-permute-start(bf16[4,32,512]{2,1,0:T(8,128)(2,1)S(1)} %get-tuple-element.7), channel_id=1, source_target_pairs={{0,7},{1,6},{2,5},{3,4},{4,3},{5,2},{6,1},{7,0},{8,15},{9,14},{10,... | collective-permute-start | bytes 393224 | tf_op jit(solution)/shard_map/ppermute | solution.py:24
  44.2 5.8 %collective-permute-start.13 = (f32[4,128,128]{2,1,0:T(8,128)S(1)}, f32[4,128,128]{2,1,0:T(8,128)S(1)}, u32[]{:S(2)}, u32[]{:S(2)}) collective-permute-start(f32[4,128,128]{2,1,0:T(8,128)S(1)} %get-tuple-element.18), channel_id=1, source_target_pairs={{8,0},{16,8},{24,16},{32,24},{40,32},{48,40},{56,48},{64,56},{72,6... | collective-permute-start | bytes 786440 | tf_op jit(solution)/shard_map/ppermute | solution.py:41
  46.6 7.7 %collective-permute-start.7 = (f32[4,128,128]{2,1,0:T(8,128)S(1)}, f32[4,128,128]{2,1,0:T(8,128)S(1)}, u32[]{:S(2)}, u32[]{:S(2)}) collective-permute-start(f32[4,128,128]{2,1,0:T(8,128)S(1)} %get-tuple-element.20), channel_id=1, source_target_pairs={{0,8},{8,16},{16,24},{24,32},{32,40},{40,48},{48,56},{56,64},{64,7... | collective-permute-start | bytes 786440 | tf_op jit(solution)/shard_map/ppermute | solution.py:40
  50.1 10.0 %collective-permute-start.14 = (f32[4,128,128]{2,1,0:T(8,128)S(1)}, f32[4,128,128]{2,1,0:T(8,128)S(1)}, u32[]{:S(2)}, u32[]{:S(2)}) collective-permute-start(f32[4,128,128]{2,1,0:T(8,128)S(1)} %add.165), channel_id=1, source_target_pairs={{16,0},{24,8},{32,16},{40,24},{48,32},{56,40},{64,48},{72,56},{80,... | collective-permute-start | bytes 786440 | tf_op jit(solution)/shard_map/ppermute | solution.py:41
  54.4 12.1 %collective-permute-start.8 = (f32[4,128,128]{2,1,0:T(8,128)S(1)}, f32[4,128,128]{2,1,0:T(8,128)S(1)}, u32[]{:S(2)}, u32[]{:S(2)}) collective-permute-start(f32[4,128,128]{2,1,0:T(8,128)S(1)} %add.152), channel_id=1, source_target_pairs={{0,16},{8,24},{16,32},{24,40},{32,48},{40,56},{48,64},{56,72},{64,... | collective-permute-start | bytes 786440 | tf_op jit(solution)/shard_map/ppermute | solution.py:40
  60.1 12.4 %collective-permute-start.15 = (f32[4,128,128]{2,1,0:T(8,128)S(1)}, f32[4,128,128]{2,1,0:T(8,128)S(1)}, u32[]{:S(2)}, u32[]{:S(2)}) collective-permute-start(f32[4,128,128]{2,1,0:T(8,128)S(1)} %add.167), channel_id=1, source_target_pairs={{32,0},{40,8},{48,16},{56,24},{64,32},{72,40},{80,48},{88,56},{96,... | collective-permute-start | bytes 786440 | tf_op jit(solution)/shard_map/ppermute | solution.py:41
  66.5 12.8 %collective-permute-start.9 = (f32[4,128,128]{2,1,0:T(8,128)S(1)}, f32[4,128,128]{2,1,0:T(8,128)S(1)}, u32[]{:S(2)}, u32[]{:S(2)}) collective-permute-start(f32[4,128,128]{2,1,0:T(8,128)S(1)} %add.154), channel_id=1, source_target_pairs={{0,32},{8,40},{16,48},{24,56},{32,64},{40,72},{48,80},{56,88},{64,... | collective-permute-start | bytes 786440 | tf_op jit(solution)/shard_map/ppermute | solution.py:40
  72.6 11.2 %collective-permute-start.16 = (f32[4,128,128]{2,1,0:T(8,128)S(1)}, f32[4,128,128]{2,1,0:T(8,128)S(1)}, u32[]{:S(2)}, u32[]{:S(2)}) collective-permute-start(f32[4,128,128]{2,1,0:T(8,128)S(1)} %add.169), channel_id=1, source_target_pairs={{64,0},{72,8},{80,16},{88,24},{96,32},{104,40},{112,48},{120,56},{... | collective-permute-start | bytes 786440 | tf_op jit(solution)/shard_map/ppermute | solution.py:41
  79.3 10.1 %collective-permute-start.10 = (f32[4,128,128]{2,1,0:T(8,128)S(1)}, f32[4,128,128]{2,1,0:T(8,128)S(1)}, u32[]{:S(2)}, u32[]{:S(2)}) collective-permute-start(f32[4,128,128]{2,1,0:T(8,128)S(1)} %add.156), channel_id=1, source_target_pairs={{0,64},{8,72},{16,80},{24,88},{32,96},{40,104},{48,112},{56,120},{... | collective-permute-start | bytes 786440 | tf_op jit(solution)/shard_map/ppermute | solution.py:40
  83.9 26.3 %collective-permute-start.17 = (f32[4,128,128]{2,1,0:T(8,128)S(1)}, f32[4,128,128]{2,1,0:T(8,128)S(1)}, u32[]{:S(2)}, u32[]{:S(2)}) collective-permute-start(f32[4,128,128]{2,1,0:T(8,128)S(1)} %add.171), channel_id=1, source_target_pairs={{128,0},{136,8},{144,16},{152,24},{160,32},{168,40},{176,48},{184,... | collective-permute-start | bytes 786440 | tf_op jit(solution)/shard_map/ppermute | solution.py:41
  89.5 22.4 %collective-permute-start.11 = (f32[4,128,128]{2,1,0:T(8,128)S(1)}, f32[4,128,128]{2,1,0:T(8,128)S(1)}, u32[]{:S(2)}, u32[]{:S(2)}) collective-permute-start(f32[4,128,128]{2,1,0:T(8,128)S(1)} %add.158), channel_id=1, source_target_pairs={{0,128},{8,136},{16,144},{24,152},{32,160},{40,168},{48,176},{56,1... | collective-permute-start | bytes 786440 | tf_op jit(solution)/shard_map/ppermute | solution.py:40
  110.2 18.7 %collective-permute-start.18 = (f32[4,128,128]{2,1,0:T(8,128)S(1)}, f32[4,128,128]{2,1,0:T(8,128)S(1)}, u32[]{:S(2)}, u32[]{:S(2)}) collective-permute-start(f32[4,128,128]{2,1,0:T(8,128)S(1)} %add.173), channel_id=1, source_target_pairs={{256,0},{264,8},{272,16},{280,24},{288,32},{296,40},{304,48},{312,... | collective-permute-start | bytes 786440 | tf_op jit(solution)/shard_map/ppermute | solution.py:41
  111.9 19.8 %collective-permute-start.12 = (f32[4,128,128]{2,1,0:T(8,128)S(1)}, f32[4,128,128]{2,1,0:T(8,128)S(1)}, u32[]{:S(2)}, u32[]{:S(2)}) collective-permute-start(f32[4,128,128]{2,1,0:T(8,128)S(1)} %add.160), channel_id=1, source_target_pairs={{0,256},{8,264},{16,272},{24,280},{32,288},{40,296},{48,304},{56,3... | collective-permute-start | bytes 786440 | tf_op jit(solution)/shard_map/ppermute | solution.py:40
